TPU v7x, 32 devices: a whole 2x2x4 slice. The times are simulated.
32 devices in a mesh: groups: 2 (over y), ctx: 4 (over z), head: 2 (over x), sub: 2 (over core).
Axes of the slice: x: 2, y: 2, z: 4, core: 2. Of those that a mesh axis runs over, the one named last changes fastest.
Arguments:
- att_query: bfloat16 [1024, 4096], P(('groups', 'ctx'), ('head', 'sub')), parts along dimension 0, may hold values from -4 to 4
- att_gate: bfloat16 [1024, 4096], P(('groups', 'ctx'), ('head', 'sub')), parts along dimension 0, may hold values from -6 to 6
- att_kv: bfloat16 [1024, 1024], P(('groups', 'ctx')), parts along dimension 0, may hold values from -4 to 4
- residual: bfloat16 [1024, 2048], P(('groups', 'ctx'), ('head', 'sub')), parts along dimension 0, may hold values from -0.19921875 to 0.19921875
- out_weight: bfloat16 [4096, 2048], P(('head', 'sub')), may hold values from -0.5 to 0.5
- norm_gain: float32 [2048], replicated, may hold values from 0.1 to 1.9
- in_weight: bfloat16 [2048, 8192], P(None, ('head', 'sub')), may hold values from -0.125 to 0.125
- beta_weight: bfloat16 [2048, 32], P(None, ('head', 'sub')), may hold values from -0.125 to 0.125
- log_decay: float32 [1024, 32], P(('groups', 'ctx'), ('head', 'sub')), parts along dimension 0, may hold values from -0.7 to 0, as said below
- delta_gain: float32 [128], replicated, may hold values from 0.1 to 1.9
Outputs:
- new_residual: bfloat16 [1024, 2048], P(('groups', 'ctx'), ('head', 'sub')), parts along dimension 0
- delta_out: bfloat16 [1024, 4096], P(('groups', 'ctx'), ('head', 'sub')), parts along dimension 0
There are 2 independent parts, one for each index of `groups`. A program takes and returns all parts, laid end to end along the dimension named above; an argument that names none is the same for every part. Nothing has to cross between parts.
Inputs may be any that keep to these rules, and one draw needn't show every extreme that they name: `log_decay`: negative.
All inputs are finite; a program needn't handle non-finite values.
Results may differ from a plain program's by a relative error of at most 0.035.
Values may be sent and summed in bfloat16 or wider, within the bound.
A program may use at most 64 MiB of HBM per device.

v0:
```python
import functools

import jax
import jax.numpy as jnp
from jax import lax
from jax.experimental import pallas as pl
from jax.experimental.pallas import tpu as pltpu
from jax.sharding import PartitionSpec as P

HEADS = 16
KV_HEADS = 2
HD = 256
DK = 128
DV = 128
EPSILON = 1e-06
NEGATIVE = -1e30
CHUNKS = 2
PIECES = 2
F32 = jnp.float32
BF16 = jnp.bfloat16
MESH = pl.DeviceIdType.MESH


def dot(a, b):
    return jnp.dot(a, b, preferred_element_type=F32)


def dot_nt(a, b):
    return lax.dot_general(a, b, (((1,), (1,)), ((), ())), preferred_element_type=F32)


def dot_tn(a, b):
    return lax.dot_general(a, b, (((0,), (0,)), ((), ())), preferred_element_type=F32)


def silu(x):
    return x * jax.nn.sigmoid(x)


def unit(x):
    return x * lax.rsqrt(jnp.sum(x * x, axis=-1, keepdims=True) + EPSILON)


def remote(src, dst, sems, index, device):
    return pltpu.make_async_remote_copy(
        src_ref=src,
        dst_ref=dst,
        send_sem=sems.at[0, index],
        recv_sem=sems.at[1, index],
        device_id=device,
        device_id_type=MESH,
    )


def kernel(
    ctx_count,
    head_count,
    query_hbm,
    gate_hbm,
    kv_hbm,
    res_hbm,
    ow_hbm,
    norm_gain_hbm,
    iw_hbm,
    bw_hbm,
    ld_hbm,
    delta_gain_hbm,
    new_res_ref,
    delta_ref,
    query_ref,
    gate_ref,
    res_ref,
    norm_gain_ref,
    bw_ref,
    ld_ref,
    delta_gain_ref,
    kv,
    ow,
    iw,
    att,
    rs_send,
    rs_recv,
    x_send,
    x_recv,
    hid,
    macc,
    trans,
    offs,
    early_in,
    late_in,
    early_out,
    late_out,
    local_out,
    read,
    load_sem,
    kv_sem,
    kvf_sem,
    rs_sem,
    x_sem,
    ag_sem,
    agf_sem,
    early_sem,
    late_sem,
):
    c = lax.axis_index("ctx")
    h = lax.axis_index("head")
    s = lax.axis_index("sub")
    rows = query_ref.shape[0]
    half = rows // 2
    heads_here = query_ref.shape[1] // HD
    shard = h * 2 + s
    width = res_ref.shape[1]
    partner = {"sub": 1 - s}
    kv_number = shard * heads_here // (HEADS // KV_HEADS)

    own_rows = pl.ds(pl.multiple_of(c * rows, rows), rows)
    loads = []
    for part in range(2):
        start = pl.multiple_of(kv_number * 2 * HD + part * HD, HD)
        loads.append(
            pltpu.make_async_copy(
                kv_hbm.at[:, pl.ds(start, HD)], kv.at[part, own_rows], load_sem.at[part]
            )
        )
    ow_load = pltpu.make_async_copy(ow_hbm, ow, load_sem.at[2])
    iw_load = pltpu.make_async_copy(iw_hbm, iw, load_sem.at[3])
    small = [
        pltpu.make_async_copy(source, target, load_sem.at[4 + i])
        for i, (source, target) in enumerate(
            [
                (query_hbm, query_ref),
                (gate_hbm, gate_ref),
                (res_hbm, res_ref),
                (norm_gain_hbm, norm_gain_ref),
                (bw_hbm, bw_ref),
                (ld_hbm, ld_ref),
                (delta_gain_hbm, delta_gain_ref),
            ]
        )
    ]
    for load in loads + small:
        load.start()

    @pl.when(c == 0)
    def _():
        early_in[...] = jnp.zeros_like(early_in)

    barrier = pltpu.get_barrier_semaphore()
    for d in range(1, ctx_count):
        pl.semaphore_signal(
            barrier, inc=1, device_id={"ctx": lax.rem(c + d, ctx_count)}, device_id_type=MESH
        )
    for d in range(1, head_count):
        pl.semaphore_signal(
            barrier, inc=1, device_id={"head": lax.rem(h + d, head_count)}, device_id_type=MESH
        )
    pl.semaphore_signal(barrier, inc=1, device_id=partner, device_id_type=MESH)
    pl.semaphore_wait(barrier, ctx_count + head_count - 1)

    sends = []
    for load in loads:
        load.wait()
    gathers = []
    for d in range(1, ctx_count):
        piece = kv.at[s, own_rows]
        copy = remote(piece, piece, kv_sem, d - 1, {"ctx": lax.rem(c + d, ctx_count)})
        copy.start()
        gathers.append(copy)
    ow_load.start()
    forwards = []
    for d in range(1, ctx_count):
        gathers[d - 1].wait_recv()
        source = lax.rem(c - d + ctx_count, ctx_count)
        piece = kv.at[s, pl.ds(pl.multiple_of(source * rows, rows), rows)]
        copy = remote(piece, piece, kvf_sem, d - 1, partner)
        copy.start()
        forwards.append(copy)
    iw_load.start()
    for copy in forwards:
        copy.wait_recv()
    sends += gathers + forwards

    for load in small:
        load.wait()

    total_rows = ctx_count * rows
    q_row = lax.broadcasted_iota(jnp.int32, (rows, total_rows), 0)
    k_row = lax.broadcasted_iota(jnp.int32, (rows, total_rows), 1)
    shift = rows.bit_length() - 1
    k_dev = k_row >> shift
    k_in = k_row & (rows - 1)
    last_block = 2 * ctx_count - 1
    q_pos = jnp.where(q_row < half, c, last_block - c) * half + (q_row & (half - 1))
    k_pos = jnp.where(k_in < half, k_dev, last_block - k_dev) * half + (k_in & (half - 1))
    visible = q_pos >= k_pos
    keys = kv[0]
    values = kv[1]
    for n in range(heads_here):
        cols = slice(n * HD, (n + 1) * HD)
        scores = dot_nt(query_ref[:, cols], keys) * (HD**-0.5)
        scores = jnp.where(visible, scores, NEGATIVE)
        weights = jnp.exp(scores - jnp.max(scores, axis=1, keepdims=True))
        total = jnp.sum(weights, axis=1, keepdims=True)
        mixed = dot(weights.astype(BF16), values) / total
        att[:, cols] = (mixed * jax.nn.sigmoid(gate_ref[:, cols].astype(F32))).astype(BF16)

    ow_load.wait()
    attended = att[...]

    def out_slice(number):
        return dot(attended, ow[:, pl.ds(pl.multiple_of(number * width, width), width)])

    chunks = [slice(k * rows // CHUNKS, (k + 1) * rows // CHUNKS) for k in range(CHUNKS)]
    peers = [lax.rem(h + 1 + i, head_count) for i in range(head_count)]
    pair_copies = []
    for i in range(head_count):
        rs_send[i] = out_slice(peers[i] * 2 + 1 - s).astype(BF16)
        copy = remote(rs_send.at[i], rs_recv.at[i], rs_sem, i, partner)
        copy.start()
        pair_copies.append(copy)
    head_copies = []
    for i in range(head_count):
        part = out_slice(peers[i] * 2 + s)
        pair_copies[i].wait_recv()
        part = part + rs_recv[i].astype(F32)
        if i < head_count - 1:
            x_send[i] = part.astype(BF16)
            for k, lines in enumerate(chunks):
                copy = remote(
                    x_send.at[i, lines], x_recv.at[i, lines], x_sem, i * CHUNKS + k, {"head": peers[i]}
                )
                copy.start()
                head_copies.append(copy)
    part = part + res_ref[...].astype(F32)
    sends += pair_copies + head_copies
    to_heads = []
    to_partner = []
    for k, lines in enumerate(chunks):
        own = part[lines]
        for i in range(head_count - 1):
            head_copies[i * CHUNKS + k].wait_recv()
            own = own + x_recv[i, lines].astype(F32)
        own16 = own.astype(BF16)
        new_res_ref[lines, :] = own16
        hid[shard, lines] = own16
        mine = hid.at[shard, lines]
        for i in range(head_count - 1):
            copy = remote(mine, mine, ag_sem, i * CHUNKS + k, {"head": peers[i]})
            copy.start()
            to_heads.append(copy)
        copy = remote(mine, mine, agf_sem, (head_count - 1) * CHUNKS + k, partner)
        copy.start()
        to_partner.append(copy)
    iw_load.wait()

    def projected(r, start):
        cols = pl.ds(pl.multiple_of(r * width, width), width)
        piece = hid[r].astype(F32)
        scaled = (piece * norm_gain_ref[:, cols]).astype(BF16)
        term = dot(scaled, iw[cols, :])
        logits = dot_nt(bw_ref[:, cols], scaled)
        square = jnp.sum(piece * piece, axis=1, keepdims=True)
        if start is None:
            macc[...] = term
            return logits, square
        macc[...] += term
        return start[0] + logits, start[1] + square

    sources = [lax.rem(h - 1 - i + head_count, head_count) * 2 for i in range(head_count - 1)]
    parts = projected(shard, None)
    for k, lines in enumerate(chunks):
        for i in range(head_count - 1):
            to_heads[k * (head_count - 1) + i].wait_recv()
            piece = hid.at[sources[i] + s, lines]
            copy = remote(piece, piece, agf_sem, i * CHUNKS + k, partner)
            copy.start()
            to_partner.append(copy)
    for copy in to_partner[:CHUNKS]:
        copy.wait_recv()
    parts = projected(h * 2 + 1 - s, parts)
    for i in range(head_count - 1):
        parts = projected(sources[i] + s, parts)
    for copy in to_partner[CHUNKS:]:
        copy.wait_recv()
    for i in range(head_count - 1):
        parts = projected(sources[i] + 1 - s, parts)
    sends += to_heads + to_partner
    scale = lax.rsqrt(parts[1] / (2 * head_count * width) + EPSILON)
    group = 2 * DK + 2 * DV
    key_here = iw.shape[1] // group
    value_here = 2 * key_here

    row = lax.broadcasted_iota(jnp.int32, (rows, rows), 0)
    col = lax.broadcasted_iota(jnp.int32, (rows, rows), 1)
    same = (row < half) == (col < half)
    on_or_below = same & (row >= col)
    strictly = same & (row > col)
    eye = jnp.where(row == col, 1.0, 0.0)
    beta = jax.nn.sigmoid(parts[0].T * scale)
    lower = jnp.where(on_or_below, 1.0, 0.0)
    every = jnp.where(same, 1.0, 0.0)
    decays = ld_ref[...]

    def row_sums(picked):
        return lax.dot_general(
            decays,
            picked,
            (((1,), (1,)), ((), ())),
            precision=lax.Precision.HIGHEST,
            preferred_element_type=F32,
        )

    cum_row = row_sums(lower)
    sum_row = row_sums(every)
    cumulative = cum_row.T
    block_sum = sum_row.T
    growth = jnp.exp(cumulative)
    carry = jnp.exp(block_sum - cumulative)

    queries, grams, attends, values_of, keys_of = [], [], [], [], []
    for j in range(key_here):
        m = macc[:, j * group : (j + 1) * group] * scale
        q = unit(silu(m[:, :DK])) * DK**-0.5
        k = unit(silu(m[:, DK : 2 * DK]))
        v = silu(m[:, 2 * DK :])
        q16, k16 = q.astype(BF16), k.astype(BF16)
        queries.append(q)
        keys_of.append(k)
        values_of += [v[:, :DV], v[:, DV:]]
        grams.append(dot_nt(k16, k16))
        attends.append(dot_nt(q16, k16))
    systems, inverses, grids = [], [], []
    for n in range(value_here):
        gap = cumulative[:, n : n + 1] - cum_row[n : n + 1, :]
        grid = jnp.where(on_or_below, jnp.exp(jnp.where(on_or_below, gap, 0.0)), 0.0)
        system = jnp.where(strictly, beta[:, n : n + 1] * grams[n // 2] * grid, 0.0)
        grids.append((attends[n // 2] * grid).astype(BF16))
        systems.append(system)
        inverses.append(eye - jnp.where((row >> 1) == (col >> 1), system, 0.0))
    level = 1
    while (1 << level) < half:
        mask = ((row >> (level + 1)) == (col >> (level + 1))) & ((row >> level) != (col >> level))
        halves = [inverse.astype(BF16) for inverse in inverses]
        firsts = [
            dot(jnp.where(mask, system, 0.0).astype(BF16), inverse).astype(BF16)
            for system, inverse in zip(systems, halves)
        ]
        inverses = [
            full - dot(inverse, product)
            for full, inverse, product in zip(inverses, halves, firsts)
        ]
        level += 1
    last = ctx_count - 1
    nxt = {"ctx": lax.min(c + 1, last)}
    prv = {"ctx": lax.max(c - 1, 0)}

    def early_copy(n):
        return remote(early_out.at[n], early_in.at[n], early_sem, n, nxt)

    def late_copy(n):
        return remote(late_out.at[n], late_in.at[n], late_sem, n, prv)

    solutions, carries = [], []
    for n in range(value_here):
        beta_n = beta[:, n : n + 1]
        right = jnp.concatenate(
            [beta_n * values_of[n], (beta_n * growth[:, n : n + 1]) * keys_of[n // 2]], axis=1
        )
        solutions.append(dot(inverses[n].astype(BF16), right.astype(BF16)).astype(BF16))
        carries.append((keys_of[n // 2] * carry[:, n : n + 1]).astype(BF16))

    def piece_rows(p):
        return slice(p * DV // PIECES, (p + 1) * DV // PIECES)

    def block_ends(n, b):
        lines = slice(b * half, (b + 1) * half)
        ends = dot_tn(solutions[n][lines], carries[n][lines])
        offs[b, n] = ends[:DV]
        whole = jnp.exp(block_sum[b * half : b * half + 1, n : n + 1])
        trans[b, n] = (whole * eye[:DK, :DK] - ends[DV:]).astype(BF16)
        if b == 0:
            for p in range(PIECES):
                early_out[n * PIECES + p] = ends[piece_rows(p)].astype(BF16)

    for n in range(value_here):
        block_ends(n, 0)

    @pl.when(c == 0)
    def _():
        for n in range(value_here * PIECES):
            early_copy(n).start()

    for n in range(value_here):
        block_ends(n, 1)
        inner = dot(grids[n], solutions[n])
        local_out[n] = inner[:, :DV]
        read[n] = (growth[:, n : n + 1] * queries[n // 2] - inner[:, DV:]).astype(BF16)

    def finish(n, b, state):
        lines = slice(b * half, (b + 1) * half)
        out = local_out[n, lines, :] + dot_nt(read[n, lines, :], state)
        mean = jnp.mean(out * out, axis=1, keepdims=True)
        out = out * lax.rsqrt(mean + EPSILON) * delta_gain_ref[...]
        if isinstance(n, int):
            delta_ref[lines, n * DV : (n + 1) * DV] = out.astype(BF16)
        else:
            delta_ref[lines, pl.ds(pl.multiple_of(n * DV, DV), DV)] = out.astype(BF16)

    def passed(n, p, b, state):
        return (dot(state, trans[b, n]) + offs[b, n, piece_rows(p), :]).astype(BF16)

    def whole_state(ref, n):
        return jnp.concatenate([ref[n * PIECES + p] for p in range(PIECES)], axis=0)

    @pl.when(c > 0)
    def _():
        def early_turn(n, carried):
            for p in range(PIECES):
                at = n * PIECES + p
                early_copy(at).wait_recv()
                end = passed(n, p, 0, early_in[at])

                @pl.when(c < last)
                def _():
                    early_out[at] = end
                    early_copy(at).start()

                @pl.when(c == last)
                def _():
                    late_in[at] = end
                    late_out[at] = passed(n, p, 1, end)
                    late_copy(at).start()

            return carried

        lax.fori_loop(0, value_here, early_turn, 0)

    for n in range(value_here):
        finish(n, 0, whole_state(early_in, n))

    @pl.when((c > 0) & (c < last))
    def _():
        def late_turn(n, carried):
            for p in range(PIECES):
                at = n * PIECES + p
                late_copy(at).wait_recv()
                late_out[at] = passed(n, p, 1, late_in[at])
                late_copy(at).start()
            return carried

        lax.fori_loop(0, value_here, late_turn, 0)

    @pl.when(c == 0)
    def _():
        def last_turn(n, carried):
            for p in range(PIECES):
                late_copy(n * PIECES + p).wait_recv()
            finish(n, 1, whole_state(late_in, n))
            return carried

        lax.fori_loop(0, value_here, last_turn, 0)

    @pl.when(c > 0)
    def _():
        for n in range(value_here):
            finish(n, 1, whole_state(late_in, n))

    for copy in sends:
        copy.wait_send()

    def drain(n, carry):
        @pl.when(c < last)
        def _():
            early_copy(n).wait_send()

        @pl.when(c > 0)
        def _():
            late_copy(n).wait_send()

        return carry

    lax.fori_loop(0, value_here * PIECES, drain, 0)


def settle(first_ref, second_ref, first_out, second_out):
    first_out[...] = first_ref[...]
    second_out[...] = second_ref[...]


def local(
    ctx_count,
    head_count,
    att_query,
    att_gate,
    att_kv,
    residual,
    out_weight,
    norm_gain,
    in_weight,
    beta_weight,
    log_decay,
    delta_gain,
):
    rows = att_query.shape[0]
    width = residual.shape[1]
    value_here = log_decay.shape[1]
    vmem = pl.BlockSpec(memory_space=pltpu.VMEM)
    hbm = pl.BlockSpec(memory_space=pl.ANY)
    heads_less = max(head_count - 1, 1)
    pair = pltpu.SemaphoreType.DMA
    outputs = pl.pallas_call(
        functools.partial(kernel, ctx_count, head_count),
        out_shape=(
            jax.ShapeDtypeStruct((rows, width), BF16),
            jax.ShapeDtypeStruct((rows, value_here * DV), BF16),
        ),
        in_specs=[hbm] * 10,
        out_specs=(vmem, vmem),
        scratch_shapes=[
            pltpu.VMEM(att_query.shape, BF16),
            pltpu.VMEM(att_gate.shape, BF16),
            pltpu.VMEM(residual.shape, BF16),
            pltpu.VMEM((1, norm_gain.shape[0]), F32),
            pltpu.VMEM(beta_weight.shape[::-1], BF16),
            pltpu.VMEM(log_decay.shape[::-1], F32),
            pltpu.VMEM((1, DV), F32),
            pltpu.VMEM((2, ctx_count * rows, HD), BF16),
            pltpu.VMEM(out_weight.shape, BF16),
            pltpu.VMEM(in_weight.shape, BF16),
            pltpu.VMEM(att_query.shape, BF16),
            pltpu.VMEM((head_count, rows, width), BF16),
            pltpu.VMEM((head_count, rows, width), BF16),
            pltpu.VMEM((heads_less, rows, width), BF16),
            pltpu.VMEM((heads_less, rows, width), BF16),
            pltpu.VMEM((2 * head_count, rows, width), BF16),
            pltpu.VMEM((rows, in_weight.shape[1]), F32),
            pltpu.VMEM((2, value_here, DK, DK), BF16),
            pltpu.VMEM((2, value_here, DK, DV), F32),
            pltpu.VMEM((value_here * PIECES, DV // PIECES, DK), BF16),
            pltpu.VMEM((value_here * PIECES, DV // PIECES, DK), BF16),
            pltpu.VMEM((value_here * PIECES, DV // PIECES, DK), BF16),
            pltpu.VMEM((value_here * PIECES, DV // PIECES, DK), BF16),
            pltpu.VMEM((value_here, rows, DV), F32),
            pltpu.VMEM((value_here, rows, DK), BF16),
            pair((11,)),
            pair((2, ctx_count)),
            pair((2, ctx_count)),
            pair((2, head_count)),
            pair((2, head_count * CHUNKS)),
            pair((2, head_count * CHUNKS)),
            pair((2, head_count * CHUNKS)),
            pair((2, value_here * PIECES)),
            pair((2, value_here * PIECES)),
        ],
        compiler_params=pltpu.CompilerParams(collective_id=0, has_side_effects=True),
    )(
        att_query,
        att_gate,
        att_kv,
        residual,
        out_weight,
        norm_gain.reshape(1, -1),
        in_weight,
        beta_weight.T,
        log_decay.T,
        delta_gain.reshape(1, -1),
    )
    return pl.pallas_call(
        settle,
        out_shape=tuple(jax.ShapeDtypeStruct(x.shape, x.dtype) for x in outputs),
        in_specs=[vmem, vmem],
        out_specs=(vmem, vmem),
    )(*outputs)


def solution(mesh):
    return jax.shard_map(
        functools.partial(local, mesh.shape["ctx"], mesh.shape["head"]),
        mesh=mesh,
        in_specs=(
            P(("groups", "ctx"), ("head", "sub")),
            P(("groups", "ctx"), ("head", "sub")),
            P(("groups", "ctx"), None),
            P(("groups", "ctx"), ("head", "sub")),
            P(("head", "sub"), None),
            P(),
            P(None, ("head", "sub")),
            P(None, ("head", "sub")),
            P(("groups", "ctx"), ("head", "sub")),
            P(),
        ),
        out_specs=(P(("groups", "ctx"), ("head", "sub")), P(("groups", "ctx"), ("head", "sub"))),
        check_vma=False,
    )
```

profile of v0, /device:TPU:0, one launch (start us, length us, event | category | flops | bytes accessed | tf_op | source)
XLA Modules:
  0.0 54.1 jit_solution(5113515942180977407)
XLA Ops:
  0.6 51.7 %shard_map.113 = (bf16[128,512]{1,0:T(8,128)(2,1)}, bf16[128,1024]{1,0:T(8,128)(2,1)}) custom-call(bf16[128,1024]{1,0:T(8,128)(2,1)} %query_hbm.1, bf16[128,1024]{1,0:T(8,128)(2,1)} %gate_hbm.1, bf16[128,1024]{1,0:T(8,128)(2,1)} %kv_hbm.1, bf16[128,512]{1,0:T(8,128)(2,1)} %res_hbm.1, bf16[1024,2048]{1,0:T(8,128)(2,1)} %ow_hbm.1, f32[1,2048]{1,0:T(1,128)} %bitcast.5, ...), custom_call_target="tpu_custom_call" | custom-call | tf_op jit(solution)/shard_map/pallas_call | solution.py:511
  52.3 1.8 %shard_map.114 = (bf16[128,512]{1,0:T(8,128)(2,1)}, bf16[128,1024]{1,0:T(8,128)(2,1)}) custom-call(bf16[128,512]{1,0:T(8,128)(2,1)} %get-tuple-element.4.first_ref, bf16[128,1024]{1,0:T(8,128)(2,1)} %get-tuple-element.5.second_ref), custom_call_target="tpu_custom_call" | custom-call | tf_op jit(solution)/shard_map/pallas_call | solution.py:568
where the time goes:
time: 54.2 us; the launch traced here: 54.1 us
  Pallas kernels  53.5 us (99%)
  between operations  0.64 us (1%)
    pallas_call x1, Pallas kernels, local(): pl.pallas_call(functools.partial(kernel, ctx_count, head_count), out_shap...  51.7 us
    pallas_call x1, Pallas kernels, local(): pl.pallas_call(settle, out_shape=tuple((jax.ShapeDtypeStruct(x.shape, x.d...  1.78 us

commit v1 on v0

v1 whole, which is shorter than its diff:
```python
import functools

import jax
import jax.numpy as jnp
from jax import lax
from jax.experimental import pallas as pl
from jax.experimental.pallas import tpu as pltpu
from jax.sharding import PartitionSpec as P

HEADS = 16
KV_HEADS = 2
HD = 256
DK = 128
DV = 128
EPSILON = 1e-06
NEGATIVE = -1e30
PIECES = 2
LATE_FROM = 1
FIRST_STOP = 4
SECOND_STOP = 10
SECOND_TWO = 6
F32 = jnp.float32
BF16 = jnp.bfloat16
MESH = pl.DeviceIdType.MESH


def dot(a, b):
    return jnp.dot(a, b, preferred_element_type=F32)


def dot_nt(a, b):
    return lax.dot_general(a, b, (((1,), (1,)), ((), ())), preferred_element_type=F32)


def dot_tn(a, b):
    return lax.dot_general(a, b, (((0,), (0,)), ((), ())), preferred_element_type=F32)


def silu(x):
    return x * jax.nn.sigmoid(x)


def unit(x):
    return x * lax.rsqrt(jnp.sum(x * x, axis=-1, keepdims=True) + EPSILON)


def remote(src, dst, sems, index, device):
    return pltpu.make_async_remote_copy(
        src_ref=src,
        dst_ref=dst,
        send_sem=sems.at[0, index],
        recv_sem=sems.at[1, index],
        device_id=device,
        device_id_type=MESH,
    )


def kernel(
    ctx_count,
    head_count,
    query_hbm,
    gate_hbm,
    kv_hbm,
    res_hbm,
    ow_hbm,
    norm_gain_hbm,
    iw_hbm,
    bw_hbm,
    ld_hbm,
    delta_gain_hbm,
    new_res_ref,
    delta_ref,
    query_ref,
    gate_ref,
    res_ref,
    norm_gain_ref,
    bw_ref,
    ld_ref,
    delta_gain_ref,
    kv_early,
    kv_late,
    ow,
    iw,
    att,
    rs_send,
    rs_recv,
    x_send,
    x_recv,
    part,
    hid,
    macc,
    grid_ref,
    growth_ref,
    carry_ref,
    whole_ref,
    trans,
    offs,
    early_in,
    late_in,
    early_out,
    late_out,
    local_out,
    read,
    load_sem,
    kv_sem,
    kvf_sem,
    rs_sem,
    x_sem,
    agf_sem,
    early_sem,
    late_sem,
):
    c = lax.axis_index("ctx")
    h = lax.axis_index("head")
    s = lax.axis_index("sub")
    rows = query_ref.shape[0]
    half = rows // 2
    heads_here = query_ref.shape[1] // HD
    width = res_ref.shape[1]
    partner = {"sub": 1 - s}
    kv_number = (h * 2 + s) * heads_here // (HEADS // KV_HEADS)
    last = ctx_count - 1
    group = 2 * DK + 2 * DV
    key_here = iw.shape[1] // group
    value_here = 2 * key_here
    kv_parts = [kv_early, kv_late]
    sends = []

    def block_rows(source):
        return pl.ds(pl.multiple_of(source * half, half), half)

    def half_rows(b):
        return slice(b * half, (b + 1) * half)

    loads = []
    for b in range(2):
        for p in range(2):
            start = pl.multiple_of(kv_number * 2 * HD + p * HD, HD)
            loads.append(
                pltpu.make_async_copy(
                    kv_hbm.at[half_rows(b), pl.ds(start, HD)],
                    kv_parts[b].at[p, block_rows(c)],
                    load_sem.at[b * 2 + p],
                )
            )
    ow_load = pltpu.make_async_copy(ow_hbm, ow, load_sem.at[4])
    iw_load = pltpu.make_async_copy(iw_hbm, iw, load_sem.at[5])
    small = [
        pltpu.make_async_copy(source, target, load_sem.at[6 + i])
        for i, (source, target) in enumerate(
            [
                (query_hbm, query_ref),
                (gate_hbm, gate_ref),
                (res_hbm, res_ref),
                (ld_hbm, ld_ref),
                (norm_gain_hbm, norm_gain_ref),
                (bw_hbm, bw_ref),
                (delta_gain_hbm, delta_gain_ref),
            ]
        )
    ]
    for load in loads + small[:2] + [ow_load] + small[2:]:
        load.start()

    barrier = pltpu.get_barrier_semaphore()
    for d in range(1, ctx_count):
        pl.semaphore_signal(
            barrier, inc=1, device_id={"ctx": lax.rem(c + d, ctx_count)}, device_id_type=MESH
        )
    for d in range(1, head_count):
        pl.semaphore_signal(
            barrier, inc=1, device_id={"head": lax.rem(h + d, head_count)}, device_id_type=MESH
        )
    pl.semaphore_signal(barrier, inc=1, device_id=partner, device_id_type=MESH)

    @pl.when(c == 0)
    def _():
        early_in[...] = jnp.zeros_like(early_in)

    for load in loads:
        load.wait()
    pl.semaphore_wait(barrier, ctx_count + head_count - 1)

    def kv_send(b, d):
        piece = kv_parts[b].at[s, block_rows(c)]
        target = {"ctx": lax.rem(c + d, ctx_count)}
        return remote(piece, piece, kv_sem, b * last + d - 1, target)

    def kv_forward(b, d):
        piece = kv_parts[b].at[s, block_rows(lax.rem(c - d + ctx_count, ctx_count))]
        return remote(piece, piece, kvf_sem, b * last + d - 1, partner)

    for d in range(1, ctx_count):

        @pl.when(c + d < ctx_count)
        def _():
            kv_send(0, d).start()

    for d in range(last, 0, -1):

        @pl.when(c + d >= ctx_count)
        def _():
            kv_send(0, d).start()
            kv_send(1, d).start()

    iw_load.start()
    for load in small:
        load.wait()

    triangle_row = lax.broadcasted_iota(jnp.int32, (half, half), 0)
    triangle_col = lax.broadcasted_iota(jnp.int32, (half, half), 1)
    causal = triangle_row >= triangle_col

    def attend(b, own, keys, values):
        for n in range(heads_here):
            cols = slice(n * HD, (n + 1) * HD)
            query = query_ref[half_rows(b), cols]
            scores = []
            for at, key in zip(own, keys):
                piece = dot_nt(query, key) * (HD**-0.5)
                if at is not None:
                    row = lax.broadcasted_iota(jnp.int32, piece.shape, 0)
                    col = lax.broadcasted_iota(jnp.int32, piece.shape, 1)
                    hidden = (col - at > row) & (col < at + half)
                    piece = jnp.where(hidden, NEGATIVE, piece)
                scores.append(piece)
            top = functools.reduce(
                jnp.maximum, [jnp.max(piece, axis=1, keepdims=True) for piece in scores]
            )
            weights = [jnp.exp(piece - top) for piece in scores]
            total = sum(jnp.sum(piece, axis=1, keepdims=True) for piece in weights)
            mixed = sum(dot(piece.astype(BF16), value) for piece, value in zip(weights, values))
            mixed = mixed / total
            gate = jax.nn.sigmoid(gate_ref[half_rows(b), cols].astype(F32))
            att[half_rows(b), cols] = (mixed * gate).astype(BF16)

    peers = [lax.rem(h + 1 + i, head_count) for i in range(head_count)]

    def shard_of(i, side):
        return peers[i] * 2 + side

    def rs_copy(b, i):
        return remote(rs_send.at[b, i], rs_recv.at[b, i], rs_sem, b * head_count + i, partner)

    def x_copy(b, d, i):
        return remote(
            x_send.at[b, i],
            x_recv.at[b, d - 1, i],
            x_sem,
            (b * max(head_count - 1, 1) + d - 1) * head_count + i,
            {"head": lax.rem(h + d, head_count)},
        )

    def out_projection(b):
        attended = att[half_rows(b), :]

        def out_slice(number):
            return dot(attended, ow[:, pl.ds(pl.multiple_of(number * width, width), width)])

        for i in range(head_count):
            rs_send[b, i] = out_slice(shard_of(i, 1 - s)).astype(BF16)
            rs_copy(b, i).start()
        for i in range(head_count):
            own = out_slice(shard_of(i, s))
            if i == head_count - 1:
                own = own + res_ref[half_rows(b), :].astype(F32)
            rs_copy(b, i).wait_recv()
            own = own + rs_recv[b, i].astype(F32)
            part[b, i] = own
            x_send[b, i] = own.astype(BF16)
            for d in range(1, head_count):
                x_copy(b, d, i).start()

    def hidden_copy(b, i):
        mine = hid.at[b, shard_of(i, s)]
        return remote(mine, mine, agf_sem, b * head_count + i, partner)

    def projection(b):
        for i in range(head_count):
            own = part[b, i]
            for d in range(1, head_count):
                j = (i + d) % head_count
                x_copy(b, d, j).wait_recv()
                own = own + x_recv[b, d - 1, j].astype(F32)
            own16 = own.astype(BF16)
            if i == head_count - 1:
                new_res_ref[half_rows(b), :] = own16
            hid[b, shard_of(i, s)] = own16
            hidden_copy(b, i).start()
            parts = projected(b, shard_of(i, s), parts if i else None)
        for i in range(head_count):
            hidden_copy(b, i).wait_recv()
            parts = projected(b, shard_of(i, 1 - s), parts)
        return parts

    def projected(b, r, start):
        cols = pl.ds(pl.multiple_of(r * width, width), width)
        piece = hid[b, r].astype(F32)
        scaled = (piece * norm_gain_ref[:, cols]).astype(BF16)
        term = dot(scaled, iw[cols, :])
        logits = dot_nt(bw_ref[:, cols], scaled)
        square = jnp.sum(piece * piece, axis=1, keepdims=True)
        if start is None:
            macc[b] = term
            return logits, square
        macc[b] += term
        return start[0] + logits, start[1] + square

    row = lax.broadcasted_iota(jnp.int32, (rows, rows), 0)
    col = lax.broadcasted_iota(jnp.int32, (rows, rows), 1)

    def masks():
        same = (row < half) == (col < half)
        return same, same & (row >= col)

    def twice(values, b, j):
        lines = half_rows(b)
        return jnp.concatenate(
            [values[lines, 2 * j : 2 * j + 1], values[lines, 2 * j + 1 : 2 * j + 2]], axis=0
        )

    def decay_tables():
        same, on_or_below = masks()
        eye = jnp.where(row == col, 1.0, 0.0)
        decays = ld_ref[...]

        def row_sums(picked):
            return lax.dot_general(
                decays,
                jnp.where(picked, 1.0, 0.0),
                (((1,), (1,)), ((), ())),
                precision=lax.Precision.HIGHEST,
                preferred_element_type=F32,
            )

        cumulative = row_sums(on_or_below).T
        block_sum = row_sums(same).T
        rest = jnp.exp(block_sum - cumulative)
        whole = jnp.exp(block_sum)
        for b in range(2):
            for j in range(key_here):
                wide = jnp.broadcast_to(twice(cumulative, b, j), (rows, rows))
                gap = wide - wide.T
                grid_ref[b, j] = jnp.where(
                    on_or_below, jnp.exp(jnp.where(on_or_below, gap, 0.0)), 0.0
                )
                growth_ref[b, j] = jnp.exp(wide)
                carry_ref[b, j] = jnp.broadcast_to(twice(rest, b, j), (rows, rows))
            for n in range(value_here):
                whole_ref[b, n] = whole[b * half : b * half + 1, n : n + 1] * eye[:DK, :DK]

    nxt = {"ctx": lax.min(c + 1, last)}
    prv = {"ctx": lax.max(c - 1, 0)}

    def early_copy(n):
        return remote(early_out.at[n], early_in.at[n], early_sem, n, nxt)

    def late_copy(n):
        return remote(late_out.at[n], late_in.at[n], late_sem, n, prv)

    def piece_rows(p):
        return slice(p * DV // PIECES, (p + 1) * DV // PIECES)

    def delta(b, parts):
        same, on_or_below = masks()
        strictly = same & (row > col)
        eye = jnp.where(row == col, 1.0, 0.0)
        scale = lax.rsqrt(parts[1] / (2 * head_count * width) + EPSILON)
        beta_all = jax.nn.sigmoid(parts[0].T * scale)

        def doubled(x):
            return jnp.concatenate([x, x], axis=0)

        queries, keys, values, betas, systems, inverses, grids = [], [], [], [], [], [], []
        for j in range(key_here):
            m = macc[b, :, j * group : (j + 1) * group] * scale
            q = doubled(unit(silu(m[:, :DK])) * DK**-0.5)
            k = doubled(unit(silu(m[:, DK : 2 * DK])))
            v = silu(m[:, 2 * DK :])
            v = jnp.concatenate([v[:, :DV], v[:, DV:]], axis=0)
            beta = jnp.concatenate(
                [beta_all[:, 2 * j : 2 * j + 1], beta_all[:, 2 * j + 1 : 2 * j + 2]], axis=0
            )
            q16, k16 = q.astype(BF16), k.astype(BF16)
            queries.append(q)
            keys.append(k)
            values.append(v)
            betas.append(beta)
            grid = grid_ref[b, j]
            system = jnp.where(strictly, beta * dot_nt(k16, k16) * grid, 0.0)
            grids.append((dot_nt(q16, k16) * grid).astype(BF16))
            systems.append(system)
            inverses.append(eye - jnp.where((row >> 1) == (col >> 1), system, 0.0))
        level = 1
        while (1 << level) < half:
            mask = ((row >> (level + 1)) == (col >> (level + 1))) & (
                (row >> level) != (col >> level)
            )
            halves = [inverse.astype(BF16) for inverse in inverses]
            firsts = [
                dot(jnp.where(mask, system, 0.0).astype(BF16), inverse).astype(BF16)
                for system, inverse in zip(systems, halves)
            ]
            inverses = [
                full - dot(inverse, product)
                for full, inverse, product in zip(inverses, halves, firsts)
            ]
            level += 1
        solutions = []
        for j in range(key_here):
            right = jnp.concatenate(
                [betas[j] * values[j], betas[j] * growth_ref[b, j] * keys[j]], axis=1
            )
            solutions.append(dot(inverses[j].astype(BF16), right.astype(BF16)).astype(BF16))
        for j in range(key_here):
            carried = (keys[j] * carry_ref[b, j]).astype(BF16)
            for i in range(2):
                n = 2 * j + i
                lines = half_rows(i)
                ends = dot_tn(solutions[j][lines], carried[lines])
                offs[b, n] = ends[:DV]
                trans[b, n] = (whole_ref[b, n] - ends[DV:]).astype(BF16)
                if b == 0:
                    for p in range(PIECES):
                        early_out[n * PIECES + p] = ends[piece_rows(p)].astype(BF16)
            if b == 0:

                @pl.when(c == 0)
                def _():
                    for at in range(2 * j * PIECES, 2 * (j + 1) * PIECES):
                        early_copy(at).start()

        for j in range(key_here):
            inner = dot(grids[j], solutions[j])
            local_out[b, j] = inner[:, :DV]
            read[b, j] = (growth_ref[b, j] * queries[j] - inner[:, DV:]).astype(BF16)

    def passed(n, p, b, state):
        return (dot(state, trans[b, n]) + offs[b, n, piece_rows(p), :]).astype(BF16)

    def early_relay(low, high):
        def early_turn(at, carried):
            n = at // PIECES
            early_copy(at).wait_recv()
            lines = pl.ds(pl.multiple_of(lax.rem(at, PIECES) * (DV // PIECES), DV // PIECES), DV // PIECES)
            end = (dot(early_in[at], trans[0, n]) + offs[0, n, lines, :]).astype(BF16)

            @pl.when(c < last)
            def _():
                early_out[at] = end
                early_copy(at).start()

            @pl.when(c == last)
            def _():
                late_in[at] = end
                late_out[at] = (dot(end, trans[1, n]) + offs[1, n, lines, :]).astype(BF16)
                late_copy(at).start()

            return carried

        lax.fori_loop(low, high, early_turn, 0)

    def finish(n, b, state):
        pair, side = n // 2, n % 2
        if isinstance(n, int):
            lines = half_rows(side)
        else:
            lines = pl.ds(pl.multiple_of(lax.rem(n, 2) * half, half), half)
        out = local_out[b, pair, lines, :] + dot_nt(read[b, pair, lines, :], state)
        mean = jnp.mean(out * out, axis=1, keepdims=True)
        out = out * lax.rsqrt(mean + EPSILON) * delta_gain_ref[...]
        if isinstance(n, int):
            delta_ref[half_rows(b), n * DV : (n + 1) * DV] = out.astype(BF16)
        else:
            delta_ref[half_rows(b), pl.ds(pl.multiple_of(n * DV, DV), DV)] = out.astype(BF16)

    def whole_state(ref, n):
        return jnp.concatenate([ref[n * PIECES + p] for p in range(PIECES)], axis=0)

    for d in range(1, ctx_count):

        @pl.when(c >= d)
        def _():
            kv_send(0, d).wait_recv()
            kv_forward(0, d).start()

    for d in range(1, ctx_count):

        @pl.when(c >= d)
        def _():
            kv_forward(0, d).wait_recv()

    for k in range(ctx_count):

        @pl.when(c == k)
        def _():
            lines = slice(0, (k + 1) * half)
            attend(0, [k * half], [kv_early[0, lines]], [kv_early[1, lines]])

    ow_load.wait()
    out_projection(0)
    decay_tables()

    def late_front(choices):
        for d in range(last, 0, -1):

            @pl.when(c < d)
            def _():
                for b in range(2):
                    kv_send(b, d).wait_recv()
                    kv_forward(b, d).start()

        for d in range(last, 0, -1):

            @pl.when(c < d)
            def _():
                for b in range(2):
                    kv_forward(b, d).wait_recv()

        for k in choices:

            @pl.when(c == k)
            def _():
                lines = slice(k * half, ctx_count * half)
                attend(
                    1,
                    [None, 0],
                    [kv_early[0], kv_late[0, lines]],
                    [kv_early[1], kv_late[1, lines]],
                )

        out_projection(1)

    @pl.when(c >= LATE_FROM)
    def _():
        late_front(range(LATE_FROM, ctx_count))

    iw_load.wait()
    delta(0, projection(0))

    @pl.when(c < LATE_FROM)
    def _():
        late_front(range(LATE_FROM))

    pieces = value_here * PIECES
    first_stop = jnp.where(c == 1, FIRST_STOP * pieces // 16, 0)
    second_stop = jnp.where(c == 1, SECOND_STOP * pieces // 16, jnp.where(c == 2, SECOND_TWO * pieces // 16, 0))
    third_stop = jnp.where(c > 0, pieces, 0)
    early_relay(0, first_stop)
    late_parts = projection(1)
    early_relay(first_stop, second_stop)
    delta(1, late_parts)
    early_relay(second_stop, third_stop)

    for n in range(value_here):
        finish(n, 0, whole_state(early_in, n))

    @pl.when((c > 0) & (c < last))
    def _():
        def late_turn(n, carried):
            for p in range(PIECES):
                at = n * PIECES + p
                late_copy(at).wait_recv()
                late_out[at] = passed(n, p, 1, late_in[at])
                late_copy(at).start()
            return carried

        lax.fori_loop(0, value_here, late_turn, 0)

    @pl.when(c == 0)
    def _():
        def last_turn(n, carried):
            for p in range(PIECES):
                late_copy(n * PIECES + p).wait_recv()
            finish(n, 1, whole_state(late_in, n))
            return carried

        lax.fori_loop(0, value_here, last_turn, 0)

    @pl.when(c > 0)
    def _():
        for n in range(value_here):
            finish(n, 1, whole_state(late_in, n))

    for d in range(1, ctx_count):
        kv_send(0, d).wait_send()
        kv_forward(0, d).wait_send()

        @pl.when(c + d >= ctx_count)
        def _():
            kv_send(1, d).wait_send()

        @pl.when(c < d)
        def _():
            kv_forward(1, d).wait_send()

    for b in range(2):
        for i in range(head_count):
            rs_copy(b, i).wait_send()
            hidden_copy(b, i).wait_send()
            for d in range(1, head_count):
                x_copy(b, d, i).wait_send()

    def drain(n, carry):
        @pl.when(c < last)
        def _():
            early_copy(n).wait_send()

        @pl.when(c > 0)
        def _():
            late_copy(n).wait_send()

        return carry

    lax.fori_loop(0, value_here * PIECES, drain, 0)


def settle(first_ref, second_ref, first_out, second_out):
    first_out[...] = first_ref[...]
    second_out[...] = second_ref[...]


def local(
    ctx_count,
    head_count,
    att_query,
    att_gate,
    att_kv,
    residual,
    out_weight,
    norm_gain,
    in_weight,
    beta_weight,
    log_decay,
    delta_gain,
):
    rows = att_query.shape[0]
    width = residual.shape[1]
    value_here = log_decay.shape[1]
    vmem = pl.BlockSpec(memory_space=pltpu.VMEM)
    hbm = pl.BlockSpec(memory_space=pl.ANY)
    heads_less = max(head_count - 1, 1)
    pair = pltpu.SemaphoreType.DMA
    outputs = pl.pallas_call(
        functools.partial(kernel, ctx_count, head_count),
        out_shape=(
            jax.ShapeDtypeStruct((rows, width), BF16),
            jax.ShapeDtypeStruct((rows, value_here * DV), BF16),
        ),
        in_specs=[hbm] * 10,
        out_specs=(vmem, vmem),
        scratch_shapes=[
            pltpu.VMEM(att_query.shape, BF16),
            pltpu.VMEM(att_gate.shape, BF16),
            pltpu.VMEM(residual.shape, BF16),
            pltpu.VMEM((1, norm_gain.shape[0]), F32),
            pltpu.VMEM(beta_weight.shape[::-1], BF16),
            pltpu.VMEM(log_decay.shape[::-1], F32),
            pltpu.VMEM((1, DV), F32),
            pltpu.VMEM((2, ctx_count * rows // 2, HD), BF16),
            pltpu.VMEM((2, ctx_count * rows // 2, HD), BF16),
            pltpu.VMEM(out_weight.shape, BF16),
            pltpu.VMEM(in_weight.shape, BF16),
            pltpu.VMEM(att_query.shape, BF16),
            pltpu.VMEM((2, head_count, rows // 2, width), BF16),
            pltpu.VMEM((2, head_count, rows // 2, width), BF16),
            pltpu.VMEM((2, head_count, rows // 2, width), BF16),
            pltpu.VMEM((2, heads_less, head_count, rows // 2, width), BF16),
            pltpu.VMEM((2, head_count, rows // 2, width), F32),
            pltpu.VMEM((2, 2 * head_count, rows // 2, width), BF16),
            pltpu.VMEM((2, rows // 2, in_weight.shape[1]), F32),
            pltpu.VMEM((2, value_here // 2, rows, rows), F32),
            pltpu.VMEM((2, value_here // 2, rows, rows), F32),
            pltpu.VMEM((2, value_here // 2, rows, rows), F32),
            pltpu.VMEM((2, value_here, DK, DK), F32),
            pltpu.VMEM((2, value_here, DK, DK), BF16),
            pltpu.VMEM((2, value_here, DV, DK), F32),
            pltpu.VMEM((value_here * PIECES, DV // PIECES, DK), BF16),
            pltpu.VMEM((value_here * PIECES, DV // PIECES, DK), BF16),
            pltpu.VMEM((value_here * PIECES, DV // PIECES, DK), BF16),
            pltpu.VMEM((value_here * PIECES, DV // PIECES, DK), BF16),
            pltpu.VMEM((2, value_here // 2, rows, DV), F32),
            pltpu.VMEM((2, value_here // 2, rows, DK), BF16),
            pair((13,)),
            pair((2, 2 * (ctx_count - 1))),
            pair((2, 2 * (ctx_count - 1))),
            pair((2, 2 * head_count)),
            pair((2, 2 * heads_less * head_count)),
            pair((2, 2 * head_count)),
            pair((2, value_here * PIECES)),
            pair((2, value_here * PIECES)),
        ],
        compiler_params=pltpu.CompilerParams(collective_id=0, has_side_effects=True),
    )(
        att_query,
        att_gate,
        att_kv,
        residual,
        out_weight,
        norm_gain.reshape(1, -1),
        in_weight,
        beta_weight.T,
        log_decay.T,
        delta_gain.reshape(1, -1),
    )
    return pl.pallas_call(
        settle,
        out_shape=tuple(jax.ShapeDtypeStruct(x.shape, x.dtype) for x in outputs),
        in_specs=[vmem, vmem],
        out_specs=(vmem, vmem),
    )(*outputs)


def solution(mesh):
    return jax.shard_map(
        functools.partial(local, mesh.shape["ctx"], mesh.shape["head"]),
        mesh=mesh,
        in_specs=(
            P(("groups", "ctx"), ("head", "sub")),
            P(("groups", "ctx"), ("head", "sub")),
            P(("groups", "ctx"), None),
            P(("groups", "ctx"), ("head", "sub")),
            P(("head", "sub"), None),
            P(),
            P(None, ("head", "sub")),
            P(None, ("head", "sub")),
            P(("groups", "ctx"), ("head", "sub")),
            P(),
        ),
        out_specs=(P(("groups", "ctx"), ("head", "sub")), P(("groups", "ctx"), ("head", "sub"))),
        check_vma=False,
    )
```

time: 54.2 us -> 49.7 us (0.917)
  Pallas kernels: 53.5 us -> 48.8 us
    pallas_call x1, Pallas kernels: 51.7 us -> 47.1 us  [local(): pl.pallas_call(functools.partial(kernel, ctx_count, head_count), out_shap...]
where the time goes in v1:
time: 49.7 us; the launch traced here: 49.5 us
  Pallas kernels  48.8 us (98%)
  between operations  0.64 us (1%)
    pallas_call x1, Pallas kernels, local(): pl.pallas_call(functools.partial(kernel, ctx_count, head_count), out_shap...  47.1 us
    pallas_call x1, Pallas kernels, local(): pl.pallas_call(settle, out_shape=tuple((jax.ShapeDtypeStruct(x.shape, x.d...  1.78 us

profile of v1, /device:TPU:0, one launch (start us, length us, event | category | flops | bytes accessed | tf_op | source)
XLA Modules:
  0.0 49.5 jit_solution(8196066961447777943)
XLA Ops:
  0.6 47.1 %shard_map.113 = (bf16[128,512]{1,0:T(8,128)(2,1)}, bf16[128,1024]{1,0:T(8,128)(2,1)}) custom-call(bf16[128,1024]{1,0:T(8,128)(2,1)} %query_hbm.1, bf16[128,1024]{1,0:T(8,128)(2,1)} %gate_hbm.1, bf16[128,1024]{1,0:T(8,128)(2,1)} %kv_hbm.1, bf16[128,512]{1,0:T(8,128)(2,1)} %res_hbm.1, bf16[1024,2048]{1,0:T(8,128)(2,1)} %ow_hbm.1, f32[1,2048]{1,0:T(1,128)} %bitcast.5, ...), custom_call_target="tpu_custom_call" | custom-call | tf_op jit(solution)/shard_map/pallas_call | solution.py:644
  47.7 1.8 %shard_map.114 = (bf16[128,512]{1,0:T(8,128)(2,1)}, bf16[128,1024]{1,0:T(8,128)(2,1)}) custom-call(bf16[128,512]{1,0:T(8,128)(2,1)} %get-tuple-element.4.first_ref, bf16[128,1024]{1,0:T(8,128)(2,1)} %get-tuple-element.5.second_ref), custom_call_target="tpu_custom_call" | custom-call | tf_op jit(solution)/shard_map/pallas_call | solution.py:706
